TPU v7x, 128 devices: a whole 4x4x4 slice. The times are simulated.
128 devices in a mesh: lon: 64 (over x, z, y_hi, core), lat: 2 (over y_lo).
Axes of the slice: x: 4, y: 4 (y_hi: 2, y_lo: 2; y = y_hi * 2 + y_lo), z: 4, core: 2. Of those that a mesh axis runs over, the one named last changes fastest.
Arguments:
- rows_in: bfloat16 [128, 4096, 256], P(('lat', 'lon')), may hold values from -6 to 6
- row_shift: int32 [128], P(('lat', 'lon')), may hold values from 0 to 4095, as said below
- kernel: float32 [9, 256], replicated, may hold values from -2 to 2
- w_in: bfloat16 [256, 1024], replicated, may hold values from -0.375 to 0.375
- w_out: bfloat16 [1024, 256], replicated, may hold values from -0.1875 to 0.1875
- cotangent: bfloat16 [128, 4096, 256], P('lat', 'lon'), may hold values from -6 to 6
Outputs:
- block_out: bfloat16 [128, 4096, 256], P('lat', 'lon')
- grad_rows: bfloat16 [128, 4096, 256], P(('lat', 'lon'))
- grad_kernel: float32 [9, 256], replicated
- grad_w_in: float32 [256, 1024], replicated
- grad_w_out: float32 [1024, 256], replicated
Inputs may be any that keep to these rules, and one draw needn't show every extreme that they name: `row_shift`: some row has rotation 0 and some row has rotation 4096 - 1.
All inputs are finite; a program needn't handle non-finite values.
Results may differ from a plain program's by a relative error of at most 0.0065.
Values may be sent and summed in bfloat16 or wider, within the bound.
A program may use at most 128 MiB of HBM per device.

v0:
```python
import math

import jax
import jax.numpy as jnp
from jax import lax
from jax.sharding import PartitionSpec as P

GELU_C = math.sqrt(2.0 / math.pi)
TAPS = [(a, b) for a in (-1, 0, 1) for b in (-1, 0, 1)]


def with_halo(cells, sides, width, closed):
    for axis, dim in sides:
        count = lax.axis_size(axis)
        ends = count if closed else count - 1
        head = lax.slice_in_dim(cells, 0, width, axis=dim)
        tail = lax.slice_in_dim(cells, cells.shape[dim] - width, cells.shape[dim], axis=dim)
        cells = jnp.concatenate(
            [
                lax.ppermute(tail, axis, [(i, (i + 1) % count) for i in range(ends)]),
                cells,
                lax.ppermute(head, axis, [((i + 1) % count, i) for i in range(ends)]),
            ],
            axis=dim,
        )
    return cells


def gelu_value(h):
    inner = GELU_C * (h + 0.044715 * h * h * h)
    return 0.5 * h * (1.0 + jnp.tanh(inner))


def gelu_slope(h):
    t = jnp.tanh(GELU_C * (h + 0.044715 * h * h * h))
    return 0.5 * (1.0 + t) + 0.5 * h * (1.0 - t * t) * GELU_C * (1.0 + 3.0 * 0.044715 * h * h)


def pad_rows(field):
    return with_halo(field, (("lat", 0),), 4, False)


def pad_columns(field):
    return with_halo(field, (("lon", 1),), 4, True)


def shards(rows_in, row_shift, kernel, w_in, w_out, cotangent):
    rows_dev, nlon, chans = rows_in.shape
    n_lon = lax.axis_size("lon")
    n_lat = lax.axis_size("lat")
    tile_cols = nlon // n_lon
    tile_rows = rows_dev * n_lon
    scale = 1.0 / math.sqrt(tile_rows * n_lat * nlon)
    column = lax.broadcasted_iota(jnp.int32, (rows_dev, nlon), 1)
    shifts = row_shift[:, None]
    shifted = jnp.take_along_axis(rows_in, ((column + shifts) % nlon)[:, :, None], axis=1)
    tile = lax.all_to_all(shifted, "lon", split_axis=1, concat_axis=0, tiled=True)
    padded = pad_rows(pad_columns(tile))
    padded_wide = padded.astype(jnp.float32)
    tile = padded[4 : 4 + tile_rows, 4 : 4 + tile_cols]
    depth = jnp.zeros((tile_rows, tile_cols, chans), jnp.float32)
    for tap, (a, b) in enumerate(TAPS):
        depth = (
            depth
            + kernel[tap]
            * padded_wide[4 + 4 * a : 4 + 4 * a + tile_rows, 4 + 4 * b : 4 + 4 * b + tile_cols]
        )
    mean = jnp.mean(depth, axis=-1, keepdims=True)
    centred = depth - mean
    rinv = lax.rsqrt(jnp.mean(centred * centred, axis=-1, keepdims=True) + 1e-06)
    nhat = centred * rinv
    pixels = tile_rows * tile_cols
    normed = nhat.astype(jnp.bfloat16).reshape(pixels, chans)
    cot_flat = cotangent.reshape(pixels, chans)
    hidden = jnp.dot(normed, w_in, preferred_element_type=jnp.float32)
    act = gelu_value(hidden).astype(jnp.bfloat16)
    mlp_out = jnp.dot(act, w_out, preferred_element_type=jnp.float32)
    block_out = (tile.astype(jnp.float32) + mlp_out.reshape(tile_rows, tile_cols, chans)).astype(
        jnp.bfloat16
    )
    g_act = jnp.dot(cot_flat, w_out.T, preferred_element_type=jnp.float32)
    g_hidden = (g_act * gelu_slope(hidden)).astype(jnp.bfloat16)
    grad_out = scale * jnp.dot(act.T, cot_flat, preferred_element_type=jnp.float32)
    grad_in = scale * jnp.dot(normed.T, g_hidden, preferred_element_type=jnp.float32)
    g_norm = jnp.dot(g_hidden, w_in.T, preferred_element_type=jnp.float32).reshape(
        tile_rows, tile_cols, chans
    )
    g_mean = jnp.mean(g_norm, axis=-1, keepdims=True)
    g_proj = jnp.mean(g_norm * nhat, axis=-1, keepdims=True)
    g_dw = (rinv * (g_norm - g_mean - nhat * g_proj)).astype(jnp.bfloat16)
    g_dw_wide = g_dw.astype(jnp.float32)
    kernel_terms = []
    for tap, (a, b) in enumerate(TAPS):
        piece = padded_wide[4 + 4 * a : 4 + 4 * a + tile_rows, 4 + 4 * b : 4 + 4 * b + tile_cols]
        kernel_terms.append(jnp.sum(piece * g_dw_wide, axis=(0, 1)))
    grad_kernel = scale * jnp.stack(kernel_terms)
    grad_kernel, grad_in, grad_out = lax.psum((grad_kernel, grad_in, grad_out), ("lon", "lat"))
    g_pad = pad_rows(pad_columns(g_dw)).astype(jnp.float32)
    g_band = cotangent.astype(jnp.float32)
    for tap, (a, b) in enumerate(TAPS):
        g_band = (
            g_band
            + kernel[tap]
            * g_pad[4 - 4 * a : 4 - 4 * a + tile_rows, 4 - 4 * b : 4 - 4 * b + tile_cols]
        )
    returned = lax.all_to_all(
        g_band.astype(jnp.bfloat16), "lon", split_axis=0, concat_axis=1, tiled=True
    )
    grad_rows = jnp.take_along_axis(returned, ((column - shifts) % nlon)[:, :, None], axis=1)
    return (block_out, grad_rows, grad_kernel, grad_in, grad_out)


def solution(mesh):
    in_specs = (
        P(("lat", "lon"), None, None),
        P(("lat", "lon")),
        P(),
        P(),
        P(),
        P("lat", "lon", None),
    )
    out_specs = (P("lat", "lon", None), P(("lat", "lon"), None, None), P(), P(), P())
    return jax.shard_map(shards, mesh=mesh, in_specs=in_specs, out_specs=out_specs, check_vma=False)
```

profile of v0, /device:TPU:1, one launch (start us, length us, event | category | flops | bytes accessed | tf_op | source)
XLA Modules:
  0.0 421.9 jit_solution(1873442955003119886)
XLA Ops:
  8.8 17.0 %gather_fusion = bf16[4096,256]{1,0:T(8,128)(2,1)} fusion(bf16[4096,256]{1,0:T(8,128)(2,1)S(1)} %bitcast.55, s32[4096]{0:T(1024)S(1)} %broadcast_clamp_fusion.1), kind=kCustom, calls=%fused_computation.clone | custom fusion | bytes 4210688 | tf_op jit(solution)/shard_map/jit(take_along_axis)/gather | solution.py:56
  27.8 25.1 %copy.15 = bf16[1,4096,256]{2,0,1:T(2,128)(2,1)} copy(bf16[1,4096,256]{2,1,0:T(8,128)(2,1)S(1)} %bitcast_select_fusion.1) | data formatting | bytes 4194304 | tf_op jit(solution)/shard_map/jit(take_along_axis)/select_n | solution.py:56
  53.3 21.6 %reduce.5 = bf16[4096,256]{1,0:T(8,128)(2,1)S(1)} reduce(bf16[4096,1,256]{2,1,0:T(2,128)(2,1)} %bitcast.61, bf16[]{:T(256)} %broadcast.231), dimensions={1}, to_apply=%bitcast.51.reduce_sub_computation | reduce | bytes 4194306
  76.9 43.0 %all_to_all.24 = bf16[64,2,8192]{2,1,0:T(2,128)(2,1)S(1)} all-to-all(bf16[64,2,8192]{2,1,0:T(2,128)(2,1)} %reshape.243), channel_id=1, replica_groups=mesh['lon'=64,'lat'=2] {'lon'}, dimensions={0} | all-to-all | bytes 4194304 | tf_op jit(solution)/shard_map/all_to_all | solution.py:57
  119.9 6.8 %reshape.244 = bf16[4096,1,256]{2,1,0:T(2,128)(2,1)} reshape(bf16[64,2,8192]{2,1,0:T(2,128)(2,1)S(1)} %all_to_all.24) | data formatting | bytes 4194304
  129.5 3.2 collective-permute-start
  136.8 4.9 %collective-permute-start.2 = (bf16[4,72,256]{2,1,0:T(8,128)(2,1)S(1)}, bf16[4,72,256]{2,1,0:T(8,128)(2,1)S(1)}, u32[]{:S(2)}, u32[]{:S(2)}) collective-permute-start(bf16[4,72,256]{2,1,0:T(8,128)(2,1)S(1)} %get-tuple-element.22), channel_id=1, source_target_pairs={{0,1},{2,3},{4,5},{6,7},{8,9},{10,11},{12,13},{14,15},{16,17},{18,... | collective-permute-start | bytes 442376 | tf_op jit(solution)/shard_map/ppermute | solution.py:20
  144.5 5.2 %fusion.29 = (f32[64,64]{1,0:T(8,128)S(1)}, f32[64,64,256]{2,1,0:T(8,128)}) fusion(f32[72,72,256]{2,1,0:T(8,128)S(1)} %maximum_convert_fusion, f32[256]{0:T(256)S(1)} %bitcast.84, f32[256]{0:T(256)S(1)} %bitcast.86, f32[256]{0:T(256)S(1)} %bitcast.72, f32[256]{0:T(256)S(1)} %bitcast.74, f32[256]{0:T(256)S(1)} %bitcast.76, f32[256]{0:T(256)S(1)} %bitcast.78, ...), kind=kLoop, calls=%fused_computation.87 | loop fusion | flops 18870272 | bytes 41968640 | tf_op jit(solution)/shard_map/reduce_sum | solution.py:68
  149.7 3.0 multiply_reduce_fusion.1
  154.7 11.2 %multiply_convert_fusion = (bf16[4096,1024]{1,0:T(8,128)(2,1)}, f32[4096,1024]{1,0:T(8,128)}) fusion(bf16[4096,256]{1,0:T(8,128)(2,1)S(1)} %bitcast.63, bf16[256,1024]{1,0:T(8,128)(2,1)S(1)} %copy-done.10), kind=kOutput, calls=%fused_computation.11 | convolution fusion | flops 2185232384 | bytes 27787264 | tf_op jit(solution)/shard_map/dot_general | solution.py:75
  165.9 13.5 %fusion.6 = bf16[4096,1024]{1,0:T(8,128)(2,1)S(1)} fusion(f32[4096,1024]{1,0:T(8,128)} %get-tuple-element.38, bf16[4096,256]{1,0:T(8,128)(2,1)S(1)} %bitcast.65, bf16[1024,256]{1,0:T(8,128)(2,1)S(1)} %copy-done.11), kind=kOutput, calls=%fused_computation.10 | convolution fusion | flops 2227175424 | bytes 27787264 | tf_op jit(solution)/shard_map/dot_general | solution.py:81
  179.4 2.6 fusion.33
  184.9 18.5 %fusion.15 = (f32[256]{0:T(256)S(1)}, f32[256]{0:T(256)S(1)}, f32[256]{0:T(256)S(1)}, f32[256]{0:T(256)S(1)}, f32[256]{0:T(256)S(1)}, /*index=5*/f32[256]{0:T(25...) fusion(f32[72,72,256]{2,1,0:T(8,128)} %copy-done.2, ...), kind=kLoop, calls=%fused_computation.29 | loop fusion | flops 27260672 | bytes 48309248 | tf_op jit(solution)/shard_map/reduce_sum | solution.py:95
  203.5 6.4 %collective-permute-start.5 = (bf16[64,4,256]{2,1,0:T(4,128)(2,1)S(1)}, bf16[64,4,256]{2,1,0:T(4,128)(2,1)S(1)}, u32[]{:S(2)}, u32[]{:S(2)}) collective-permute-start(bf16[64,4,256]{2,1,0:T(4,128)(2,1)S(1)} %get-tuple-element.25), channel_id=1, source_target_pairs={{2,0},{4,2},{6,4},{8,6},{10,8},{12,10},{14,12},{16,14},{18,16},{20... | collective-permute-start | bytes 393224 | tf_op jit(solution)/shard_map/ppermute | solution.py:22
  214.6 4.1 collective-permute-start.6
  218.7 6.8 %convolution_multiply_fusion = f32[1024,256]{1,0:T(8,128)} fusion(bf16[4096,1024]{1,0:T(8,128)(2,1)} %get-tuple-element.37, bf16[4096,256]{1,0:T(8,128)(2,1)S(1)} %bitcast.66), kind=kOutput, calls=%fused_computation.60 | convolution fusion | flops 2147745792 | bytes 11534336 | tf_op jit(solution)/shard_map/dot_general | solution.py:83
  226.7 5.9 %fusion.17 = bf16[64,64,256]{2,1,0:T(8,128)(2,1)} fusion(f32[72,72,256]{2,1,0:T(8,128)S(1)} %maximum_convert_fusion.1, bf16[64,64,256]{2,1,0:T(8,128)(2,1)S(1)} %copy-done.8, f32[256]{0:T(256)S(1)} %bitcast.85, f32[256]{0:T(256)S(1)} %bitcast.87, f32[256]{0:T(256)S(1)} %bitcast.73, f32[256]{0:T(256)S(1)} %bitcast.75, f32[256]{0:T(256)S(1)} %bitcast.77, ...), kind=kLoop, calls=%fused_computation.32 | loop fusion | flops 20971520 | bytes 41952256 | tf_op jit(solution)/shard_map/convert_element_type | solution.py:107
  232.6 12.2 %all-to-all-start.1 = ((bf16[64,64,256]{2,1,0:T(8,128)(2,1)}), bf16[64,64,256]{2,1,0:T(8,128)(2,1)}, u32[]{:S(2)}, u32[]{:S(2)}) async-start(bf16[64,64,256]{2,1,0:T(8,128)(2,1)} %fusion.17), calls=%async_computation.1 | async-start | bytes 4194304 | tf_op jit(solution)/shard_map/all_to_all | solution.py:106
  245.1 7.4 %convolution_multiply_fusion.1 = f32[256,1024]{1,0:T(8,128)} fusion(bf16[4096,256]{1,0:T(8,128)(2,1)} %bitcast.64, bf16[4096,1024]{1,0:T(8,128)(2,1)} %copy-done.4), kind=kOutput, calls=%fused_computation.61 | convolution fusion | flops 2147745792 | bytes 11534336 | tf_op jit(solution)/shard_map/dot_general | solution.py:84
  252.5 5.8 %fusion.34 = f32[4096,256]{1,0:T(8,128)S(1)} fusion(bf16[4096,1024]{1,0:T(8,128)(2,1)} %get-tuple-element.37, bf16[1024,256]{1,0:T(8,128)(2,1)S(1)} %copy-done.11), kind=kOutput, calls=%fused_computation.93 | convolution fusion | flops 2147483648 | bytes 13107200 | tf_op jit(solution)/shard_map/dot_general | solution.py:77
  260.5 68.5 %psum.21 = f32[9,256]{1,0:T(8,128)} all-reduce(f32[9,256]{1,0:T(8,128)S(1)} %broadcast_multiply_fusion.2), channel_id=1, replica_groups=mesh['lon'=64,'lat'=2] {'lon','lat'}, use_global_device_ids=true, to_apply=%region_13.15 | all-reduce | flops 2304 | bytes 18432 | tf_op jit(solution)/shard_map/psum | solution.py:97
  329.0 17.9 %gather_fusion.1 = bf16[4096,256]{1,0:T(8,128)(2,1)} fusion(bf16[4096,256]{1,0:T(8,128)(2,1)} %bitcast.18, s32[4096]{0:T(1024)S(1)} %broadcast_clamp_fusion), kind=kCustom, calls=%fused_computation.1.clone | custom fusion | bytes 4210688 | tf_op jit(solution)/shard_map/jit(take_along_axis)/gather | solution.py:109
  347.0 2.9 bitcast_select_fusion
  349.9 60.4 %all-reduce.3.cloned.1.call-done = (f32[256,1024]{1,0:T(8,128)}, f32[1024,256]{1,0:T(8,128)}) async-done(((f32[256,1024]{1,0:T(8,128)}, f32[1024,256]{1,0:T(8,128)}), (f32[256,1024]{1,0:T(8,128)}, f32[1024,256]{1,0:T(8,128)})) %all-reduce.3.cloned.1.call-update) | async-done | bytes 2097168 | tf_op jit(solution)/shard_map/psum | solution.py:97
  (67 shorter events, 32.8 us)
Async XLA Ops:
  7.2 1.6 copy-start
  126.7 15.0 %copy-start.9 = (f32[9,256]{1,0:T(8,128)S(1)}, f32[9,256]{1,0:T(8,128)}, u32[]{:S(2)}) copy-start(f32[9,256]{1,0:T(8,128)} %param.10) | copy-start | bytes 27652
  129.3 6.0 %collective-permute-start.1 = (bf16[64,4,256]{2,1,0:T(4,128)(2,1)S(1)}, bf16[64,4,256]{2,1,0:T(4,128)(2,1)S(1)}, u32[]{:S(2)}, u32[]{:S(2)}) collective-permute-start(bf16[64,4,256]{2,1,0:T(4,128)(2,1)S(1)} %get-tuple-element.27), channel_id=1, source_target_pairs={{2,0},{4,2},{6,4},{8,6},{10,8},{12,10},{14,12},{16,14},{18,16},{20... | collective-permute-start | bytes 393224 | tf_op jit(solution)/shard_map/ppermute | solution.py:22
  129.5 5.9 %collective-permute-start = (bf16[64,4,256]{2,1,0:T(4,128)(2,1)S(1)}, bf16[64,4,256]{2,1,0:T(4,128)(2,1)S(1)}, u32[]{:S(2)}, u32[]{:S(2)}) collective-permute-start(bf16[64,4,256]{2,1,0:T(4,128)(2,1)S(1)} %get-tuple-element.26), channel_id=1, source_target_pairs={{0,2},{2,4},{4,6},{6,8},{8,10},{10,12},{12,14},{14,16},{16,18},{18... | collective-permute-start | bytes 393224 | tf_op jit(solution)/shard_map/ppermute | solution.py:20
  135.5 6.3 %collective-permute-start.3 = (bf16[4,72,256]{2,1,0:T(8,128)(2,1)S(1)}, bf16[4,72,256]{2,1,0:T(8,128)(2,1)S(1)}, u32[]{:S(2)}, u32[]{:S(2)}) collective-permute-start(bf16[4,72,256]{2,1,0:T(8,128)(2,1)S(1)} %get-tuple-element.23), channel_id=1, source_target_pairs={{1,0},{3,2},{5,4},{7,6},{9,8},{11,10},{13,12},{15,14},{17,16},{19,... | collective-permute-start | bytes 442376 | tf_op jit(solution)/shard_map/ppermute | solution.py:22
  136.8 6.5 %collective-permute-start.2 = (bf16[4,72,256]{2,1,0:T(8,128)(2,1)S(1)}, bf16[4,72,256]{2,1,0:T(8,128)(2,1)S(1)}, u32[]{:S(2)}, u32[]{:S(2)}) collective-permute-start(bf16[4,72,256]{2,1,0:T(8,128)(2,1)S(1)} %get-tuple-element.22), channel_id=1, source_target_pairs={{0,1},{2,3},{4,5},{6,7},{8,9},{10,11},{12,13},{14,15},{16,17},{18,... | collective-permute-start | bytes 442376 | tf_op jit(solution)/shard_map/ppermute | solution.py:20
  144.5 5.2 %copy-start.2 = (f32[72,72,256]{2,1,0:T(8,128)}, f32[72,72,256]{2,1,0:T(8,128)S(1)}, u32[]{:S(2)}) copy-start(f32[72,72,256]{2,1,0:T(8,128)S(1)} %maximum_convert_fusion) | copy-start | bytes 15925252
  149.7 3.4 copy-start.3
  152.8 1.8 copy-start.10
  154.6 11.2 %copy-start.6 = (bf16[64,64,256]{2,1,0:T(8,128)(2,1)}, bf16[64,64,256]{2,1,0:T(8,128)(2,1)S(1)}, u32[]{:S(2)}) copy-start(bf16[64,64,256]{2,1,0:T(8,128)(2,1)S(1)} %fusion.26) | copy-start | bytes 6291460
  154.6 11.2 %copy-start.7 = (bf16[64,64,256]{2,1,0:T(8,128)(2,1)S(1)}, bf16[64,64,256]{2,1,0:T(8,128)(2,1)}, u32[]{:S(2)}) copy-start(bf16[64,64,256]{2,1,0:T(8,128)(2,1)} %param.13) | copy-start | bytes 6291460
  154.7 11.2 %copy-start.11 = (bf16[1024,256]{1,0:T(8,128)(2,1)S(1)}, bf16[1024,256]{1,0:T(8,128)(2,1)}, u32[]{:S(2)}) copy-start(bf16[1024,256]{1,0:T(8,128)(2,1)} %param.12) | copy-start | bytes 1572868
  179.3 3.2 copy-start.4
  182.6 2.2 copy-start.5
  184.9 33.9 %copy-start.8 = (bf16[64,64,256]{2,1,0:T(8,128)(2,1)S(1)}, bf16[64,64,256]{2,1,0:T(8,128)(2,1)}, u32[]{:S(2)}) copy-start(bf16[64,64,256]{2,1,0:T(8,128)(2,1)} %param.13) | copy-start | bytes 6291460
  203.5 7.4 %collective-permute-start.5 = (bf16[64,4,256]{2,1,0:T(4,128)(2,1)S(1)}, bf16[64,4,256]{2,1,0:T(4,128)(2,1)S(1)}, u32[]{:S(2)}, u32[]{:S(2)}) collective-permute-start(bf16[64,4,256]{2,1,0:T(4,128)(2,1)S(1)} %get-tuple-element.25), channel_id=1, source_target_pairs={{2,0},{4,2},{6,4},{8,6},{10,8},{12,10},{14,12},{16,14},{18,16},{20... | collective-permute-start | bytes 393224 | tf_op jit(solution)/shard_map/ppermute | solution.py:22
  209.9 3.3 collective-permute-start.4
  213.3 12.2 %collective-permute-start.7 = (bf16[4,72,256]{2,1,0:T(8,128)(2,1)S(1)}, bf16[4,72,256]{2,1,0:T(8,128)(2,1)S(1)}, u32[]{:S(2)}, u32[]{:S(2)}) collective-permute-start(bf16[4,72,256]{2,1,0:T(8,128)(2,1)S(1)} %get-tuple-element.21), channel_id=1, source_target_pairs={{1,0},{3,2},{5,4},{7,6},{9,8},{11,10},{13,12},{15,14},{17,16},{19,... | collective-permute-start | bytes 442376 | tf_op jit(solution)/shard_map/ppermute | solution.py:22
  214.6 10.9 %collective-permute-start.6 = (bf16[4,72,256]{2,1,0:T(8,128)(2,1)S(1)}, bf16[4,72,256]{2,1,0:T(8,128)(2,1)S(1)}, u32[]{:S(2)}, u32[]{:S(2)}) collective-permute-start(bf16[4,72,256]{2,1,0:T(8,128)(2,1)S(1)} %get-tuple-element.20), channel_id=1, source_target_pairs={{0,1},{2,3},{4,5},{6,7},{8,9},{10,11},{12,13},{14,15},{16,17},{18,... | collective-permute-start | bytes 442376 | tf_op jit(solution)/shard_map/ppermute | solution.py:20
  232.6 96.5 %all-to-all-start.1 = ((bf16[64,64,256]{2,1,0:T(8,128)(2,1)}), bf16[64,64,256]{2,1,0:T(8,128)(2,1)}, u32[]{:S(2)}, u32[]{:S(2)}) async-start(bf16[64,64,256]{2,1,0:T(8,128)(2,1)} %fusion.17), calls=%async_computation.1 | async-start | bytes 4194304 | tf_op jit(solution)/shard_map/all_to_all | solution.py:106
  244.8 165.5 %all-reduce.3.cloned.1.call-start = ((), (), s32[]{:S(2)}) async-start(), calls=%async_computation.2 | async-start | bytes 4194304 | tf_op jit(solution)/shard_map/psum | solution.py:97
  329.0 85.8 %copy-start.1 = (bf16[1,4096,256]{2,1,0:T(8,128)(2,1)S(1)}, bf16[1,4096,256]{2,1,0:T(8,128)(2,1)}, u32[]{:S(2)}) copy-start(bf16[1,4096,256]{2,1,0:T(8,128)(2,1)} %param.8) | copy-start | bytes 6291460
Sparse Core Ops, SparseCore 0:
  252.6 157.6 all-reduce.2
where the time goes:
time: 430 us; the launch traced here: 422 us
  blocking collectives  111 us (26%)
  local copies, waits for them, and re-layouts  78.4 us (18%)
  other arithmetic  67.9 us (16%)
  waiting for transfers between devices  67.9 us (16%)
  matrix products  47.1 us (11%)
  starting transfers between devices  33.8 us (8%)
  between operations  15.4 us (4%)
    psum x1, blocking collectives, shards(): lax.psum((grad_kernel, grad_in, grad_out), ('lon', 'lat'))  68.5 us
    psum x1, waiting for transfers between devices, shards(): lax.psum((grad_kernel, grad_in, grad_out), ('lon', 'lat'))  60.4 us
    all_to_all x1, blocking collectives, shards(): lax.all_to_all(shifted, 'lon', split_axis=1, concat_axis=0, tiled=True)  43 us
    select_n x1, local copies, waits for them, and re-layouts, shards(): jnp.take_along_axis(rows_in, ((column + shifts) % nlon)[:, :, None], axis=1)  25.1 us
    unnamed x1, other arithmetic  21.6 us
    reduce_sum x1, other arithmetic, shards(): kernel_terms.append(jnp.sum(piece * g_dw_wide, axis=(0, 1)))  18.5 us
    unnamed x30, local copies, waits for them, and re-layouts  18 us
    gather x1, local copies, waits for them, and re-layouts, shards(): jnp.take_along_axis(returned, ((column - shifts) % nlon)[:, :, None], axi...  17.9 us
  transfers between devices with their start and end apart: 10, of which 7 were waited for; matrix products, arithmetic and copies ran while one was open for 10% of the time, Pallas kernels for 0%

commit v1 on v0

v1 whole, which is shorter than its diff:
```python
import functools
import math

import jax
import jax.numpy as jnp
from jax import lax
from jax.experimental import pallas as pl
from jax.experimental.pallas import tpu as pltpu
from jax.sharding import PartitionSpec as P

MESH = pl.DeviceIdType.MESH
GELU_C = math.sqrt(2.0 / math.pi)
GELU_A = 0.044715
EPS = 1e-06
F32 = jnp.float32
BF16 = jnp.bfloat16

NLON = 4096
C = 256
FF = 1024
DEVS = 64
CHAINS = 4
ROWS = 16
COLS = 64
WIDE = COLS + 8
CHUNK = 512
STEP_ROWS = CHUNK // COLS


def dot(a, b):
    return jnp.dot(a, b, preferred_element_type=F32)


def dot_t(a, b):
    return lax.dot_general(a, b, (((1,), (1,)), ((), ())), preferred_element_type=F32)


def xor4(a, b):
    return lax.rem(a + b, 2) + 2 * lax.rem(a // 2 + b // 2, 2)


def slide(ref, start, rows):
    first = lax.div(start, 8)
    off = start - 8 * first
    tiles = ref[pl.ds(first, rows // 8 + 3)]
    for by in (4, 2, 1):
        count = tiles.shape[0] - 1
        place = lax.broadcasted_iota(jnp.int32, (count, 8, C), 1)
        moved = pltpu.roll(tiles, 8 - by, 1)
        bit = jnp.full((count, 8, C), lax.rem(lax.div(off, by), 2), jnp.int32)
        tiles = jnp.where(bit == 1, jnp.where(place < 8 - by, moved[:-1], moved[1:]), tiles[:-1])
    return tiles.reshape(rows, C)


def phase_key(u):
    return 2 * lax.rem(u, 2) + u // 2


def block_kernel(
    shift_ref, rows_hbm, taps, w_in_hbm, w_out_hbm, cot_hbm,
    out_hbm, back_hbm, grads_out, gk_out,
    rowb, rowf, pieces, chain, cotv, w_in, w_out, wide, nhat, rinv, normed, gn, gdp, ghalo_s, ghalo_r,
    strip, outv, gw, gsend, grecv, rs_send, rs_recv, lat_send, lat_recv, ag, gk_mine, gk_lat, gk_all,
    load_sem, fwd_send, fwd_recv, halo_send, halo_recv, gh_send, gh_recv, bwd_send, bwd_recv, out_sem, self_sem,
    core_send, core_recv, rs_ssem, rs_rsem, lat_ssem, lat_rsem, ag_ssem, ag_rsem, full_ssem, full_rsem,
    gkl_ssem, gkl_rsem, gka_ssem, gka_rsem,
):
    me = lax.axis_index("lon")
    lat = lax.axis_index("lat")
    x = me // 16
    z = lax.rem(me // 4, 4)
    cls = lax.rem(me, 4)
    core = lax.rem(me, 2)
    chip = me // 2
    other_lat = (me, 1 - lat)
    other_core = (me + 1 - 2 * core, lat)

    def remote(src, dst, ssem, rsem, device):
        return pltpu.make_async_remote_copy(
            src_ref=src, dst_ref=dst, send_sem=ssem, recv_sem=rsem, device_id=device, device_id_type=MESH
        )

    def peer(s, k):
        m = lax.rem(5 * s, 16)
        return lax.rem(x + m // 4, 4) * 16 + lax.rem(z + lax.rem(m, 4), 4) * 4 + xor4(cls, k)

    barrier = pltpu.get_barrier_semaphore()

    def greet(s, _):
        pl.semaphore_signal(barrier, inc=1, device_id=(lax.rem(me + s, DEVS), lat), device_id_type=MESH)
        return 0

    load_rows = pltpu.make_async_copy(rows_hbm, rowb, load_sem.at[0])
    load_rows.start()
    lax.fori_loop(1, DEVS, greet, 0)
    pl.semaphore_signal(barrier, inc=1, device_id=other_lat, device_id_type=MESH)
    load_w_in = pltpu.make_async_copy(w_in_hbm, w_in, load_sem.at[1])
    load_w_out = pltpu.make_async_copy(w_out_hbm, w_out, load_sem.at[2])
    load_w_in.start()
    load_w_out.start()
    for q in range(CHAINS):
        pltpu.make_async_copy(cot_hbm.at[:, q], cotv.at[q], load_sem.at[3 + q]).start()

    no_row = 17 * lat
    for q in range(CHAINS):
        chain[q, no_row] = jnp.zeros((WIDE, C), BF16)

    def zero_gdp(r, _):
        for b in range(2):
            gdp[b, r] = jnp.zeros((WIDE + 8, C), F32)
        return 0

    lax.fori_loop(0, ROWS + 2, zero_gdp, 0)

    def zero_gw(r, _):
        for g in range(2):
            gw[g, pl.ds(pl.multiple_of(r * 16, 16), 16)] = jnp.zeros((16, FF), F32)
        return 0

    lax.fori_loop(0, 16, zero_gw, 0)

    load_rows.wait()

    def widen(r, _):
        rowf[pl.ds(8 * r, 8)] = rowb[pl.ds(pl.multiple_of(r * 64, 64), 64)].astype(F32).reshape(8, 8, C)
        return 0

    lax.fori_loop(0, NLON // 64, widen, 0)
    rowf[NLON // 8 : NLON // 8 + 12] = rowb[:96].astype(F32).reshape(12, 8, C)
    shift = shift_ref[0]

    def cut(target):
        start = lax.rem(target * COLS + (NLON - 4) + shift, NLON)
        pieces[target] = slide(rowf, start, WIDE).astype(BF16)

    pl.semaphore_wait(barrier, DEVS)

    my_slot = 1 + me // 4
    cut(me)
    own = pltpu.make_async_copy(pieces.at[me], chain.at[cls, my_slot], self_sem.at[0])
    own.start()

    def send_piece(n, _):
        target = peer(lax.rem(n, 16), phase_key(n // 16))
        cut(target)
        remote(pieces.at[target], chain.at[cls, my_slot], fwd_send, fwd_recv.at[cls], (target, lat)).start()
        return 0

    lax.fori_loop(1, DEVS, send_piece, 0)

    edge = ROWS - (ROWS - 1) * lat
    beside = 17 * (1 - lat)

    def halo_copy(q):
        return remote(chain.at[q, edge], chain.at[q, 17 * lat], halo_send.at[q], halo_recv.at[q], other_lat)

    def halo_arrived(q):
        remote(chain.at[q, edge], chain.at[q, beside], halo_send.at[q], halo_recv.at[q], other_lat).wait_recv()

    def arrive(first, q):
        count = ROWS - 1 if first else ROWS
        some = chain.at[q, pl.ds(1, count)]
        remote(some, some, fwd_send, fwd_recv.at[q], other_lat).wait_recv()
        halo_copy(q).start()

    own.wait()
    arrive(True, cls)
    load_w_in.wait()
    load_w_out.wait()
    for q in range(CHAINS):
        pltpu.make_async_copy(cot_hbm.at[:, q], cotv.at[q], load_sem.at[3 + q]).wait()

    def forward(q):
        def to_wide(r, _):
            wide[r] = chain[q, r].astype(F32)
            return 0

        lax.fori_loop(0, ROWS + 2, to_wide, 0)

        def row(t, _):
            depth = None
            for a in range(3):
                for b in range(3):
                    term = taps[3 * a + b : 3 * a + b + 1, :] * wide[t + a, 4 * b : 4 * b + COLS, :]
                    depth = term if depth is None else depth + term
            mean = jnp.mean(depth, axis=-1, keepdims=True)
            centred = depth - mean
            r = lax.rsqrt(jnp.mean(centred * centred, axis=-1, keepdims=True) + EPS)
            n = centred * r
            nhat[t] = n
            rinv[t] = jnp.broadcast_to(r, (COLS, 128))
            normed[t] = n.astype(BF16)
            return 0

        lax.fori_loop(0, ROWS, row, 0)

    def mlp(q):
        def step(h, _):
            at = pl.ds(h * STEP_ROWS, STEP_ROWS)
            nb = normed[at].reshape(CHUNK, C)
            cb = cotv[q, at].reshape(CHUNK, C)
            nbt = nb.T
            cbt = cb.T
            mlp_out = None
            g_norm = None
            for f in range(FF // 256):
                cols = slice(256 * f, 256 * f + 256)
                hid = dot(nb, w_in[:, cols])
                g_act = dot_t(cb, w_out[cols, :])
                h2 = hid * hid
                t = jnp.tanh(hid * (GELU_C + (GELU_C * GELU_A) * h2))
                p = 0.5 + 0.5 * t
                value = hid * p
                slope = p + value * (0.5 - 0.5 * t) * (2.0 * GELU_C + (6.0 * GELU_A * GELU_C) * h2)
                act = value.astype(BF16)
                g_hid = (g_act * slope).astype(BF16)
                out_part = dot(act, w_out[cols, :])
                norm_part = dot_t(g_hid, w_in[:, cols])
                mlp_out = out_part if mlp_out is None else mlp_out + out_part
                g_norm = norm_part if g_norm is None else g_norm + norm_part
                gw[0, :, cols] += dot(nbt, g_hid)
                gw[1, :, cols] += dot(cbt, act)
            gn[at] = g_norm.reshape(STEP_ROWS, COLS, C)
            centre = wide[pl.ds(1 + h * STEP_ROWS, STEP_ROWS), 4 : 4 + COLS, :]
            outv[q, at] = (centre + mlp_out.reshape(STEP_ROWS, COLS, C)).astype(BF16)
            return 0

        lax.fori_loop(0, ROWS // STEP_ROWS, step, 0)
        pltpu.make_async_copy(outv.at[q], out_hbm.at[:, q], out_sem.at[q]).start()

    def norm_back(q, buf, sums):
        def row(t, sums):
            n = nhat[t]
            g = gn[t]
            g_mean = jnp.mean(g, axis=-1, keepdims=True)
            g_proj = jnp.mean(g * n, axis=-1, keepdims=True)
            g_dw = (rinv[t][:, :1] * (g - g_mean - n * g_proj)).astype(BF16)
            wide_g = g_dw.astype(F32)
            gdp[buf, t + 1, 8 : 8 + COLS, :] = wide_g
            new = []
            for a in range(3):
                for b in range(3):
                    prod = wide[t + a, 4 * b : 4 * b + COLS, :] * wide_g
                    new.append(sums[3 * a + b] + jnp.sum(prod.reshape(COLS // 8, 8, C), axis=0))
            return tuple(new)

        sums = lax.fori_loop(0, ROWS, row, sums)
        ghalo_s[q] = gdp[buf, edge, 8 : 8 + COLS, :].astype(BF16)
        return sums

    def ghalo_copy(q):
        return remote(ghalo_s.at[q], ghalo_r.at[q], gh_send.at[q], gh_recv.at[q], other_lat)

    def back_row(q, buf, target):
        t = target // 4
        acc = None
        for a in range(3):
            for b in range(3):
                term = taps[3 * a + b : 3 * a + b + 1, :] * gdp[buf, t + 2 - a, 8 - 4 * b : 8 - 4 * b + WIDE, :]
                acc = term if acc is None else acc + term
        strip[...] = acc
        strip[4 : 4 + COLS, :] = strip[4 : 4 + COLS, :] + cotv[q, t].astype(F32)
        pieces[target] = strip[...].astype(BF16)

    def conv_back(u, q, buf):
        remote(ghalo_s.at[q], ghalo_r.at[q], gh_send.at[q], gh_recv.at[q], other_lat).wait_recv()
        gdp[buf, beside, 8 : 8 + COLS, :] = ghalo_r[q].astype(F32)

        def send(s, _):
            target = peer(s, phase_key(u))
            back_row(q, buf, target)
            remote(pieces.at[target], back_hbm.at[me], bwd_send, bwd_recv, (target, lat)).start()
            return 0

        @pl.when(u == 0)
        def _():
            back_row(q, buf, me)
            pltpu.make_async_copy(pieces.at[me], back_hbm.at[me], self_sem.at[1]).start()

        @pl.when(u > 0)
        def _():
            send(0, 0)

        lax.fori_loop(1, ROWS, send, 0)

    def chain_step(u, sums):
        q = xor4(cls, phase_key(u))
        buf = lax.rem(u, 2)
        halo_arrived(q)
        forward(q)

        @pl.when(u < CHAINS - 1)
        def _():
            arrive(False, xor4(cls, phase_key(u + 1)))

        mlp(q)
        sums = norm_back(q, buf, sums)
        ghalo_copy(q).start()

        @pl.when(u == 1)
        def _():
            remote(pieces.at[pl.ds(1, DEVS - 1)], pieces.at[pl.ds(1, DEVS - 1)], fwd_send, fwd_recv.at[0], other_lat).wait_send()

        @pl.when(u > 0)
        def _():
            conv_back(u - 1, xor4(cls, phase_key(u - 1)), 1 - buf)

        return sums

    sums = lax.fori_loop(0, CHAINS, chain_step, tuple(jnp.zeros((8, C), F32) for _ in range(9)))

    def halve(dst, src):
        def go(r, _):
            dst[r] = src[pl.ds(pl.multiple_of(r * 8, 8), 8), :].astype(BF16)
            return 0

        lax.fori_loop(0, 32, go, 0)

    halve(gsend, gw.at[1 - core])
    core_copy = remote(gsend, grecv, core_send, core_recv, other_core)
    core_copy.start()
    for j in range(9):
        gk_mine[j : j + 1, :] = jnp.sum(sums[j], axis=0, keepdims=True)
    gk_lat_copy = remote(gk_mine, gk_lat, gkl_ssem, gkl_rsem, other_lat)
    gk_lat_copy.start()

    conv_back(CHAINS - 1, xor4(cls, phase_key(CHAINS - 1)), (CHAINS - 1) % 2)

    core_copy.wait()

    def pair(r, _):
        s = gw[core, pl.ds(pl.multiple_of(r * 8, 8), 8), :] + grecv[r].astype(F32)
        rs_send[r] = s.astype(BF16)
        return 0

    lax.fori_loop(0, 32, pair, 0)

    def chip_peer(s):
        m = lax.rem(11 * s, 32)
        yh = lax.rem(chip + m, 2)
        xz = lax.rem(chip // 2 + m // 2 , 16)
        return xz * 2 + yh

    def rs_go(s, _):
        p = chip_peer(s)
        remote(rs_send.at[p], rs_recv.at[chip], rs_ssem, rs_rsem, (2 * p + core, lat)).start()
        return 0

    lax.fori_loop(1, 32, rs_go, 0)

    gk_lat_copy.wait()
    gk_all[me] = gk_mine[...] + gk_lat[...]

    def gk_go(s, _):
        p = lax.rem(me + s, DEVS)
        remote(gk_all.at[me], gk_all.at[me], gka_ssem, gka_rsem, (p, lat)).start()
        return 0

    lax.fori_loop(1, DEVS, gk_go, 0)

    rs_all = rs_send.at[pl.ds(1, 31)]
    remote(rs_all, rs_recv.at[pl.ds(1, 31)], rs_ssem, rs_rsem, other_lat).wait()
    rs_recv[chip] = rs_send[chip]

    def rs_sum(r, s):
        return s + rs_recv[r].astype(F32)

    lat_send[...] = lax.fori_loop(0, 32, rs_sum, jnp.zeros((8, FF), F32))
    lat_copy = remote(lat_send, lat_recv, lat_ssem, lat_rsem, other_lat)
    lat_copy.start()
    lat_copy.wait()
    ag[core, chip] = (lat_send[...] + lat_recv[...]).astype(BF16)

    def ag_go(s, _):
        p = chip_peer(s)
        remote(ag.at[core, chip], ag.at[core, chip], ag_ssem, ag_rsem, (2 * p + core, lat)).start()
        return 0

    lax.fori_loop(1, 32, ag_go, 0)
    ag_all = ag.at[core, pl.ds(1, 31)]
    remote(ag_all, ag_all, ag_ssem, ag_rsem, other_lat).wait()
    full = remote(ag.at[core], ag.at[core], full_ssem, full_rsem, other_core)
    full.start()
    gk_rest = gk_all.at[pl.ds(1, DEVS - 1)]
    remote(gk_rest, gk_rest, gka_ssem, gka_rsem, other_lat).wait()

    def gk_sum(r, s):
        return s + gk_all[r]

    gk_out[...] = lax.fori_loop(0, DEVS, gk_sum, jnp.zeros((16, C), F32))
    full.wait()
    save = pltpu.make_async_copy(ag, grads_out, self_sem.at[2])
    save.start()

    pltpu.make_async_copy(pieces.at[me], back_hbm.at[me], self_sem.at[1]).wait()
    for q in range(CHAINS):
        halo_copy(q).wait_send()
        ghalo_copy(q).wait_send()
        pltpu.make_async_copy(outv.at[q], out_hbm.at[:, q], out_sem.at[q]).wait()
    back_rest = back_hbm.at[pl.ds(1, DEVS - 1)]
    remote(pieces.at[pl.ds(1, DEVS - 1)], back_rest, bwd_send, bwd_recv, other_lat).wait()
    save.wait()


def finish_kernel(shift_ref, scale, back, out_tmp, grads, gk, rows_ref, out_ref, gwi_ref, gwo_ref, gk_ref, full, sem):
    copy = pltpu.make_async_copy(out_tmp, out_ref, sem)
    copy.start()
    span = 256
    full[0] = jnp.zeros((8, C), F32)

    def gather(j, _):
        piece = back[j].astype(F32).reshape(9, 8, C)
        full[8 * j] += piece[0]
        full[pl.ds(8 * j + 1, 8)] = piece[1:]
        return 0

    lax.fori_loop(0, DEVS, gather, 0)
    seam = full[0] + full[NLON // 8]
    full[0] = seam
    full[NLON // 8] = seam
    full[NLON // 8 + 1 : NLON // 8 + 4 + span // 8] = full[1 : 4 + span // 8]
    shift = shift_ref[0]

    def emit(r, _):
        start = lax.rem(r * span + NLON - shift, NLON) + 4
        rows_ref[pl.ds(pl.multiple_of(r * span, span), span), :] = slide(full, start, span).astype(BF16)
        return 0

    lax.fori_loop(0, NLON // span, emit, 0)
    gwi_ref[...] = scale * grads[0].reshape(C, FF).astype(F32)
    gwo_ref[...] = (scale * grads[1].reshape(C, FF).astype(F32)).T
    gk_ref[...] = scale * gk[:9]
    copy.wait()


def shards(rows_in, row_shift, kernel, w_in, w_out, cotangent):
    hbm = pl.BlockSpec(memory_space=pltpu.HBM)
    vmem = pl.BlockSpec(memory_space=pltpu.VMEM)
    smem = pl.BlockSpec(memory_space=pltpu.SMEM)
    dma = pltpu.SemaphoreType.DMA
    v = pltpu.VMEM
    out_tmp, back, grads, gk = pl.pallas_call(
        block_kernel,
        out_shape=(
            jax.ShapeDtypeStruct((ROWS, CHAINS, COLS, C), BF16),
            jax.ShapeDtypeStruct((DEVS, WIDE, C), BF16),
            jax.ShapeDtypeStruct((2, 32, 8, FF), BF16),
            jax.ShapeDtypeStruct((16, C), F32),
        ),
        in_specs=[smem, hbm, vmem, hbm, hbm, hbm],
        out_specs=(hbm, hbm, hbm, vmem),
        scratch_shapes=[
            v((NLON, C), BF16), v((NLON // 8 + 12, 8, C), F32), v((DEVS, WIDE, C), BF16),
            v((CHAINS, ROWS + 2, WIDE, C), BF16), v((CHAINS, ROWS, COLS, C), BF16),
            v((C, FF), BF16), v((FF, C), BF16), v((ROWS + 2, WIDE, C), F32),
            v((ROWS, COLS, C), F32), v((ROWS, COLS, 128), F32), v((ROWS, COLS, C), BF16),
            v((ROWS, COLS, C), F32), v((2, ROWS + 2, WIDE + 8, C), F32),
            v((CHAINS, COLS, C), BF16), v((CHAINS, COLS, C), BF16), v((WIDE, C), F32),
            v((CHAINS, ROWS, COLS, C), BF16), v((2, C, FF), F32),
            v((32, 8, FF), BF16), v((32, 8, FF), BF16), v((32, 8, FF), BF16), v((32, 8, FF), BF16),
            v((8, FF), F32), v((8, FF), F32), v((2, 32, 8, FF), BF16),
            v((16, C), F32), v((16, C), F32), v((DEVS, 16, C), F32),
            dma((7,)), dma, dma((4,)), dma((4,)), dma((4,)), dma((4,)), dma((4,)), dma, dma, dma((4,)), dma((3,)),
            dma, dma, dma, dma, dma, dma, dma, dma, dma, dma, dma, dma, dma, dma,
        ],
        compiler_params=pltpu.CompilerParams(
            collective_id=0, has_side_effects=True, vmem_limit_bytes=58 << 20
        ),
        name="block",
    )(row_shift, rows_in[0], kernel, w_in, w_out, cotangent.reshape(ROWS, CHAINS, COLS, C))
    scale = 1.0 / math.sqrt(2 * DEVS * NLON)
    rows, out, grad_in, grad_out, grad_kernel = pl.pallas_call(
        lambda shift_ref, *refs: finish_kernel(shift_ref, scale, *refs),
        out_shape=(
            jax.ShapeDtypeStruct((NLON, C), BF16),
            jax.ShapeDtypeStruct((ROWS, CHAINS, COLS, C), BF16),
            jax.ShapeDtypeStruct((C, FF), F32),
            jax.ShapeDtypeStruct((FF, C), F32),
            jax.ShapeDtypeStruct((9, C), F32),
        ),
        in_specs=[smem, vmem, hbm, vmem, vmem],
        out_specs=(vmem, hbm, vmem, vmem, vmem),
        scratch_shapes=[v((NLON // 8 + 36, 8, C), F32), dma],
        compiler_params=pltpu.CompilerParams(vmem_limit_bytes=40 << 20),
        name="finish",
    )(row_shift, back, out_tmp, grads, gk)
    return (
        out.reshape(ROWS * CHAINS, COLS, C),
        rows[None],
        grad_kernel,
        grad_in,
        grad_out,
    )


def solution(mesh):
    in_specs = (
        P(("lat", "lon"), None, None),
        P(("lat", "lon")),
        P(),
        P(),
        P(),
        P("lat", "lon", None),
    )
    out_specs = (P("lat", "lon", None), P(("lat", "lon"), None, None), P(), P(), P())
    return jax.shard_map(shards, mesh=mesh, in_specs=in_specs, out_specs=out_specs, check_vma=False)
```

time: 430 us -> 145 us (0.34); the launches traced: 422 us -> 144 us
  Pallas kernels: 0 us -> 138 us
  blocking collectives: 111 us -> 0 us
  local copies, waits for them, and re-layouts: 78.4 us -> 5.19 us
  other arithmetic: 67.9 us -> 0 us
  waiting for transfers between devices: 67.9 us -> 0 us
  matrix products: 47.1 us -> 0 us
  starting transfers between devices: 33.8 us -> 0 us
  between operations: 15.4 us -> 1.3 us
    pallas_call x0 -> x2, Pallas kernels: none -> 138 us  [the longest x1 133 us: shards(): pl.pallas_call(block_kernel, out_shape=(jax.ShapeDtypeStruct((ROWS, CHAIN...]
    psum x1 -> x0, blocking collectives: 68.5 us -> none  [shards(): lax.psum((grad_kernel, grad_in, grad_out), ('lon', 'lat'))]
    psum x1 -> x0, waiting for transfers between devices: 60.4 us -> none  [shards(): lax.psum((grad_kernel, grad_in, grad_out), ('lon', 'lat'))]
    dot_general x6 -> x0, matrix products: 47.1 us -> none  [the longest x1 13.5 us: shards(): g_act = jnp.dot(cot_flat, w_out.T, preferred_element_type=jnp.float32)]
    all_to_all x1 -> x0, blocking collectives: 43 us -> none  [shards(): lax.all_to_all(shifted, 'lon', split_axis=1, concat_axis=0, tiled=True)]
    gather x2 -> x0, local copies, waits for them, and re-layouts: 35 us -> none  [the longest x1 17.9 us: shards(): jnp.take_along_axis(returned, ((column - shifts) % nlon)[:, :, None], axi...]
    reduce_sum x4 -> x0, other arithmetic: 29 us -> none  [the longest x1 18.5 us: shards(): kernel_terms.append(jnp.sum(piece * g_dw_wide, axis=(0, 1)))]
    select_n x1 -> x0, local copies, waits for them, and re-layouts: 25.1 us -> none  [shards(): jnp.take_along_axis(rows_in, ((column + shifts) % nlon)[:, :, None], axis=1)]
  transfers between devices with their start and end apart: 10 -> 0, of which waited for: 7 -> 0; matrix products, arithmetic and copies ran while one was open for 10% -> 0% of each run, Pallas kernels for 0% -> 0%
where the time goes in v1:
time: 145 us; the launch traced here: 144 us
  Pallas kernels  138 us (95%)
  local copies, waits for them, and re-layouts  5.19 us (4%)
    pallas_call x1, Pallas kernels, shards(): pl.pallas_call(block_kernel, out_shape=(jax.ShapeDtypeStruct((ROWS, CHAIN...  133 us
    unnamed x8, local copies, waits for them, and re-layouts  5.19 us
    pallas_call x1, Pallas kernels, shards(): pl.pallas_call(lambda shift_ref, *refs: finish_kernel(shift_ref, scale, *...  4.58 us

profile of v1, /device:TPU:1, one launch (start us, length us, event | category | flops | bytes accessed | tf_op | source)
XLA Modules:
  0.0 144.5 jit_solution(4566451577749214282)
XLA Ops:
  1.3 133.4 %block.1 = (bf16[16,4,64,256]{3,2,1,0:T(8,128)(2,1)}, bf16[64,72,256]{2,1,0:T(8,128)(2,1)}, bf16[2,32,8,1024]{3,2,1,0:T(8,128)(2,1)}, f32[16,256]{1,0:T(8,128)}) custom-call(s32[1]{0:T(128)S(6)} %copy.11.shift_ref, bf16[4096,256]{1,0:T(8,128)(2,1)} %bitcast.4, f32[9,256]{1,0:T(8,128)} %taps.1, bf16[256,1024]{1,0:T(8,128)(2,1)} %w_in_hbm.1, ...), custom_call_target="tpu_custom_call" | custom-call | tf_op jit(solution)/shard_map/block/pallas_call | solution.py:442
  134.7 0.0 copy-start
  134.7 1.7 %copy-done = bf16[64,72,256]{2,1,0:T(8,128)(2,1)S(1)} copy-done((bf16[64,72,256]{2,1,0:T(8,128)(2,1)S(1)}, bf16[64,72,256]{2,1,0:T(8,128)(2,1)}, u32[]{:S(2)}) %copy-start) | copy-done | bytes 2359320
  136.4 0.0 copy-start.1
  136.4 1.6 %copy-done.1 = bf16[16,4,64,256]{3,2,1,0:T(8,128)(2,1)S(1)} copy-done((bf16[16,4,64,256]{3,2,1,0:T(8,128)(2,1)S(1)}, bf16[16,4,64,256]{3,2,1,0:T(8,128)(2,1)}, u32[]{:S(2)}) %copy-start.1) | copy-done | bytes 2097176
  137.9 0.0 copy-start.2
  138.0 1.2 copy-done.2
  139.2 0.0 copy-start.3
  139.2 0.7 copy-done.3
  139.9 4.6 %finish.1 = (bf16[4096,256]{1,0:T(8,128)(2,1)}, bf16[16,4,64,256]{3,2,1,0:T(8,128)(2,1)}, f32[256,1024]{1,0:T(8,128)}, f32[1024,256]{1,0:T(8,128)}, f32[9,256]{1,0:T(8,128)}) custom-call(s32[1]{0:T(128)S(6)} %copy.11.shift_ref, bf16[64,72,256]{2,1,0:T(8,128)(2,1)S(1)} %copy-done, bf16[16,4,64,256]{3,2,1,0:T(8,128)(2,1)S(1)} %copy-done.1, ...), custom_call_target="tpu_custom_call" | custom-call | tf_op jit(solution)/shard_map/finish/pallas_call | solution.py:472
Async XLA Ops:
  134.7 1.7 %copy-start = (bf16[64,72,256]{2,1,0:T(8,128)(2,1)S(1)}, bf16[64,72,256]{2,1,0:T(8,128)(2,1)}, u32[]{:S(2)}) copy-start(bf16[64,72,256]{2,1,0:T(8,128)(2,1)} %get-tuple-element.14.refs_0_) | copy-start | bytes 7077892
  136.4 1.6 %copy-start.1 = (bf16[16,4,64,256]{3,2,1,0:T(8,128)(2,1)S(1)}, bf16[16,4,64,256]{3,2,1,0:T(8,128)(2,1)}, u32[]{:S(2)}) copy-start(bf16[16,4,64,256]{3,2,1,0:T(8,128)(2,1)} %get-tuple-element.15.refs_1_) | copy-start | bytes 6291460
  137.9 1.2 copy-start.2
  139.2 0.7 copy-start.3

commit v2 on v1

--- a/solution.py
+++ b/solution.py
@@ -42,7 +42,7 @@
 def slide(ref, start, rows):
     first = lax.div(start, 8)
     off = start - 8 * first
-    tiles = ref[pl.ds(first, rows // 8 + 3)]
+    tiles = ref[pl.ds(first, rows // 8 + 3)].astype(F32)
     for by in (4, 2, 1):
         count = tiles.shape[0] - 1
         place = lax.broadcasted_iota(jnp.int32, (count, 8, C), 1)
@@ -53,13 +53,13 @@
 
 
 def phase_key(u):
-    return 2 * lax.rem(u, 2) + u // 2
+    return 2 * lax.rem(u + u // 2, 2) + u // 2
 
 
 def block_kernel(
     shift_ref, rows_hbm, taps, w_in_hbm, w_out_hbm, cot_hbm,
     out_hbm, back_hbm, grads_out, gk_out,
-    rowb, rowf, pieces, chain, cotv, w_in, w_out, wide, nhat, rinv, normed, gn, gdp, ghalo_s, ghalo_r,
+    rowb, pieces, back_pieces, chain, cotv, w_in, w_out, wide, nhat, rinv, normed, gn, gdp, ghalo_s, ghalo_r,
     strip, outv, gw, gsend, grecv, rs_send, rs_recv, lat_send, lat_recv, ag, gk_mine, gk_lat, gk_all,
     load_sem, fwd_send, fwd_recv, halo_send, halo_recv, gh_send, gh_recv, bwd_send, bwd_recv, out_sem, self_sem,
     core_send, core_recv, rs_ssem, rs_rsem, lat_ssem, lat_rsem, ag_ssem, ag_rsem, full_ssem, full_rsem,
@@ -80,9 +80,15 @@
             src_ref=src, dst_ref=dst, send_sem=ssem, recv_sem=rsem, device_id=device, device_id_type=MESH
         )
 
-    def peer(s, k):
+    def place(s):
         m = lax.rem(5 * s, 16)
-        return lax.rem(x + m // 4, 4) * 16 + lax.rem(z + lax.rem(m, 4), 4) * 4 + xor4(cls, k)
+        return lax.rem(x + m // 4, 4), lax.rem(z + lax.rem(m, 4), 4)
+
+    def chain_at(x, z, cls, u):
+        return xor4(xor4(cls, phase_key(u)), 2 * lax.rem(x + z, 2))
+
+    def chain_of(u):
+        return chain_at(x, z, cls, u)
 
     barrier = pltpu.get_barrier_semaphore()
 
@@ -90,10 +96,44 @@
         pl.semaphore_signal(barrier, inc=1, device_id=(lax.rem(me + s, DEVS), lat), device_id_type=MESH)
         return 0
 
-    load_rows = pltpu.make_async_copy(rows_hbm, rowb, load_sem.at[0])
+    load_rows = pltpu.make_async_copy(rows_hbm, rowb.at[pl.ds(0, NLON // 8)], load_sem.at[0])
+    load_wrap = pltpu.make_async_copy(rows_hbm.at[pl.ds(0, 12)], rowb.at[pl.ds(NLON // 8, 12)], load_sem.at[7])
     load_rows.start()
+    load_wrap.start()
     lax.fori_loop(1, DEVS, greet, 0)
     pl.semaphore_signal(barrier, inc=1, device_id=other_lat, device_id_type=MESH)
+    load_rows.wait()
+    load_wrap.wait()
+    shift = shift_ref[0]
+
+    def cut(target):
+        start = lax.rem(target * COLS + (NLON - 4) + shift, NLON)
+        pieces[target] = slide(rowb, start, WIDE).astype(BF16)
+
+    pl.semaphore_wait(barrier, DEVS)
+
+    my_slot = 1 + me // 4
+
+    def send_phase(u):
+        def send(s, _):
+            tx, tz = place(s)
+            target = tx * 16 + tz * 4 + chain_at(tx, tz, cls, u)
+            cut(target)
+
+            @pl.when(target != me)
+            def _():
+                remote(pieces.at[target], chain.at[cls, my_slot], fwd_send, fwd_recv.at[cls], (target, lat)).start()
+
+            @pl.when(target == me)
+            def _():
+                pltpu.make_async_copy(pieces.at[me], chain.at[cls, my_slot], self_sem.at[0]).start()
+
+            return 0
+
+        lax.fori_loop(0, ROWS, send, 0)
+
+    send_phase(0)
+
     load_w_in = pltpu.make_async_copy(w_in_hbm, w_in, load_sem.at[1])
     load_w_out = pltpu.make_async_copy(w_out_hbm, w_out, load_sem.at[2])
     load_w_in.start()
@@ -119,35 +159,6 @@
 
     lax.fori_loop(0, 16, zero_gw, 0)
 
-    load_rows.wait()
-
-    def widen(r, _):
-        rowf[pl.ds(8 * r, 8)] = rowb[pl.ds(pl.multiple_of(r * 64, 64), 64)].astype(F32).reshape(8, 8, C)
-        return 0
-
-    lax.fori_loop(0, NLON // 64, widen, 0)
-    rowf[NLON // 8 : NLON // 8 + 12] = rowb[:96].astype(F32).reshape(12, 8, C)
-    shift = shift_ref[0]
-
-    def cut(target):
-        start = lax.rem(target * COLS + (NLON - 4) + shift, NLON)
-        pieces[target] = slide(rowf, start, WIDE).astype(BF16)
-
-    pl.semaphore_wait(barrier, DEVS)
-
-    my_slot = 1 + me // 4
-    cut(me)
-    own = pltpu.make_async_copy(pieces.at[me], chain.at[cls, my_slot], self_sem.at[0])
-    own.start()
-
-    def send_piece(n, _):
-        target = peer(lax.rem(n, 16), phase_key(n // 16))
-        cut(target)
-        remote(pieces.at[target], chain.at[cls, my_slot], fwd_send, fwd_recv.at[cls], (target, lat)).start()
-        return 0
-
-    lax.fori_loop(1, DEVS, send_piece, 0)
-
     edge = ROWS - (ROWS - 1) * lat
     beside = 17 * (1 - lat)
 
@@ -157,14 +168,24 @@
     def halo_arrived(q):
         remote(chain.at[q, edge], chain.at[q, beside], halo_send.at[q], halo_recv.at[q], other_lat).wait_recv()
 
-    def arrive(first, q):
-        count = ROWS - 1 if first else ROWS
-        some = chain.at[q, pl.ds(1, count)]
-        remote(some, some, fwd_send, fwd_recv.at[q], other_lat).wait_recv()
+    def arrive(u):
+        q = chain_of(u)
+
+        @pl.when(q == cls)
+        def _():
+            some = chain.at[q, pl.ds(1, ROWS - 1)]
+            remote(some, some, fwd_send, fwd_recv.at[q], other_lat).wait_recv()
+            pltpu.make_async_copy(pieces.at[me], chain.at[cls, my_slot], self_sem.at[0]).wait()
+
+        @pl.when(q != cls)
+        def _():
+            some = chain.at[q, pl.ds(1, ROWS)]
+            remote(some, some, fwd_send, fwd_recv.at[q], other_lat).wait_recv()
+
         halo_copy(q).start()
 
-    own.wait()
-    arrive(True, cls)
+    arrive(0)
+    send_phase(1)
     load_w_in.wait()
     load_w_out.wait()
     for q in range(CHAINS):
@@ -260,72 +281,73 @@
                 acc = term if acc is None else acc + term
         strip[...] = acc
         strip[4 : 4 + COLS, :] = strip[4 : 4 + COLS, :] + cotv[q, t].astype(F32)
-        pieces[target] = strip[...].astype(BF16)
-
-    def conv_back(u, q, buf):
+        back_pieces[target] = strip[...].astype(BF16)
+
+    def conv_back(q, buf):
         remote(ghalo_s.at[q], ghalo_r.at[q], gh_send.at[q], gh_recv.at[q], other_lat).wait_recv()
         gdp[buf, beside, 8 : 8 + COLS, :] = ghalo_r[q].astype(F32)
 
         def send(s, _):
-            target = peer(s, phase_key(u))
+            tx, tz = place(s)
+            target = tx * 16 + tz * 4 + q
             back_row(q, buf, target)
-            remote(pieces.at[target], back_hbm.at[me], bwd_send, bwd_recv, (target, lat)).start()
+
+            @pl.when(target != me)
+            def _():
+                remote(back_pieces.at[target], back_hbm.at[me], bwd_send, bwd_recv, (target, lat)).start()
+
+            @pl.when(target == me)
+            def _():
+                pltpu.make_async_copy(back_pieces.at[me], back_hbm.at[me], self_sem.at[1]).start()
+
             return 0
 
-        @pl.when(u == 0)
-        def _():
-            back_row(q, buf, me)
-            pltpu.make_async_copy(pieces.at[me], back_hbm.at[me], self_sem.at[1]).start()
-
-        @pl.when(u > 0)
-        def _():
-            send(0, 0)
-
-        lax.fori_loop(1, ROWS, send, 0)
+        lax.fori_loop(0, ROWS, send, 0)
 
     def chain_step(u, sums):
-        q = xor4(cls, phase_key(u))
+        q = chain_of(u)
         buf = lax.rem(u, 2)
         halo_arrived(q)
         forward(q)
 
-        @pl.when(u < CHAINS - 1)
+        @pl.when(u > 0)
         def _():
-            arrive(False, xor4(cls, phase_key(u + 1)))
+            conv_back(chain_of(u - 1), 1 - buf)
 
         mlp(q)
+        arrive(u + 1)
         sums = norm_back(q, buf, sums)
         ghalo_copy(q).start()
 
-        @pl.when(u == 1)
+        @pl.when(u < CHAINS - 2)
         def _():
-            remote(pieces.at[pl.ds(1, DEVS - 1)], pieces.at[pl.ds(1, DEVS - 1)], fwd_send, fwd_recv.at[0], other_lat).wait_send()
-
-        @pl.when(u > 0)
-        def _():
-            conv_back(u - 1, xor4(cls, phase_key(u - 1)), 1 - buf)
+            send_phase(u + 2)
 
         return sums
 
-    sums = lax.fori_loop(0, CHAINS, chain_step, tuple(jnp.zeros((8, C), F32) for _ in range(9)))
-
-    def halve(dst, src):
-        def go(r, _):
-            dst[r] = src[pl.ds(pl.multiple_of(r * 8, 8), 8), :].astype(BF16)
-            return 0
-
-        lax.fori_loop(0, 32, go, 0)
-
-    halve(gsend, gw.at[1 - core])
+    last = CHAINS - 1
+    sums = lax.fori_loop(0, last, chain_step, tuple(jnp.zeros((8, C), F32) for _ in range(9)))
+    q = chain_of(last)
+    halo_arrived(q)
+    forward(q)
+    conv_back(chain_of(last - 1), (last - 1) % 2)
+    mlp(q)
+
+    def halve(r, _):
+        gsend[r] = gw[1 - core, pl.ds(pl.multiple_of(r * 8, 8), 8), :].astype(BF16)
+        return 0
+
+    lax.fori_loop(0, 32, halve, 0)
     core_copy = remote(gsend, grecv, core_send, core_recv, other_core)
     core_copy.start()
+
+    sums = norm_back(q, last % 2, sums)
+    ghalo_copy(q).start()
     for j in range(9):
         gk_mine[j : j + 1, :] = jnp.sum(sums[j], axis=0, keepdims=True)
     gk_lat_copy = remote(gk_mine, gk_lat, gkl_ssem, gkl_rsem, other_lat)
     gk_lat_copy.start()
 
-    conv_back(CHAINS - 1, xor4(cls, phase_key(CHAINS - 1)), (CHAINS - 1) % 2)
-
     core_copy.wait()
 
     def pair(r, _):
@@ -338,7 +360,7 @@
     def chip_peer(s):
         m = lax.rem(11 * s, 32)
         yh = lax.rem(chip + m, 2)
-        xz = lax.rem(chip // 2 + m // 2 , 16)
+        xz = lax.rem(chip // 2 + m // 2, 16)
         return xz * 2 + yh
 
     def rs_go(s, _):
@@ -348,15 +370,27 @@
 
     lax.fori_loop(1, 32, rs_go, 0)
 
+    places = (x, z, cls)
+
+    def gk_device(stage, other):
+        at = [other if stage == n else places[n] for n in range(3)]
+        return (at[0] * 16 + at[1] * 4 + at[2], lat)
+
+    def gk_start(stage, value):
+        mine = places[stage]
+        gk_all[stage, mine] = value
+        for n in range(1, 4):
+            slot = gk_all.at[stage, mine]
+            remote(slot, slot, gka_ssem.at[stage], gka_rsem.at[stage], gk_device(stage, lax.rem(mine + n, 4))).start()
+
+    def gk_end(stage):
+        some = gk_all.at[stage, pl.ds(0, 3)]
+        remote(some, some, gka_ssem.at[stage], gka_rsem.at[stage], other_lat).wait()
+        return (gk_all[stage, 0] + gk_all[stage, 1]) + (gk_all[stage, 2] + gk_all[stage, 3])
+
+    conv_back(q, last % 2)
     gk_lat_copy.wait()
-    gk_all[me] = gk_mine[...] + gk_lat[...]
-
-    def gk_go(s, _):
-        p = lax.rem(me + s, DEVS)
-        remote(gk_all.at[me], gk_all.at[me], gka_ssem, gka_rsem, (p, lat)).start()
-        return 0
-
-    lax.fori_loop(1, DEVS, gk_go, 0)
+    gk_start(0, gk_mine[...] + gk_lat[...])
 
     rs_all = rs_send.at[pl.ds(1, 31)]
     remote(rs_all, rs_recv.at[pl.ds(1, 31)], rs_ssem, rs_rsem, other_lat).wait()
@@ -368,6 +402,7 @@
     lat_send[...] = lax.fori_loop(0, 32, rs_sum, jnp.zeros((8, FF), F32))
     lat_copy = remote(lat_send, lat_recv, lat_ssem, lat_rsem, other_lat)
     lat_copy.start()
+    gk_start(1, gk_end(0))
     lat_copy.wait()
     ag[core, chip] = (lat_send[...] + lat_recv[...]).astype(BF16)
 
@@ -377,60 +412,102 @@
         return 0
 
     lax.fori_loop(1, 32, ag_go, 0)
+    gk_start(2, gk_end(1))
     ag_all = ag.at[core, pl.ds(1, 31)]
     remote(ag_all, ag_all, ag_ssem, ag_rsem, other_lat).wait()
     full = remote(ag.at[core], ag.at[core], full_ssem, full_rsem, other_core)
     full.start()
-    gk_rest = gk_all.at[pl.ds(1, DEVS - 1)]
-    remote(gk_rest, gk_rest, gka_ssem, gka_rsem, other_lat).wait()
-
-    def gk_sum(r, s):
-        return s + gk_all[r]
-
-    gk_out[...] = lax.fori_loop(0, DEVS, gk_sum, jnp.zeros((16, C), F32))
+    save_mine = pltpu.make_async_copy(ag.at[core], grads_out.at[core], self_sem.at[2])
+    save_mine.start()
+    gk_out[...] = gk_end(2)
     full.wait()
-    save = pltpu.make_async_copy(ag, grads_out, self_sem.at[2])
-    save.start()
-
-    pltpu.make_async_copy(pieces.at[me], back_hbm.at[me], self_sem.at[1]).wait()
+    save_other = pltpu.make_async_copy(ag.at[1 - core], grads_out.at[1 - core], self_sem.at[3])
+    save_other.start()
+
+    pltpu.make_async_copy(back_pieces.at[me], back_hbm.at[me], self_sem.at[1]).wait()
     for q in range(CHAINS):
         halo_copy(q).wait_send()
         ghalo_copy(q).wait_send()
         pltpu.make_async_copy(outv.at[q], out_hbm.at[:, q], out_sem.at[q]).wait()
+    fwd_rest = pieces.at[pl.ds(1, DEVS - 1)]
+    remote(fwd_rest, fwd_rest, fwd_send, fwd_recv.at[0], other_lat).wait_send()
     back_rest = back_hbm.at[pl.ds(1, DEVS - 1)]
-    remote(pieces.at[pl.ds(1, DEVS - 1)], back_rest, bwd_send, bwd_recv, other_lat).wait()
-    save.wait()
-
-
-def finish_kernel(shift_ref, scale, back, out_tmp, grads, gk, rows_ref, out_ref, gwi_ref, gwo_ref, gk_ref, full, sem):
-    copy = pltpu.make_async_copy(out_tmp, out_ref, sem)
-    copy.start()
+    remote(back_pieces.at[pl.ds(1, DEVS - 1)], back_rest, bwd_send, bwd_recv, other_lat).wait()
+    save_mine.wait()
+    save_other.wait()
+
+
+def finish_kernel(
+    shift_ref, scale, back, out_tmp, grads, gk, rows_ref, out_ref, gwi_ref, gwo_ref, gk_ref,
+    backv, gradv, gkv, rowsv, outv, gwiv, gwov, full, in_sem, out_sem, sem,
+):
+    groups = 8
+    each = DEVS // groups
     span = 256
+
+    def load(g):
+        at = pl.ds(g * each, each)
+        return pltpu.make_async_copy(back.at[at], backv.at[at], in_sem.at[g])
+
+    for g in range(groups):
+        load(g).start()
+    load_grads = pltpu.make_async_copy(grads, gradv, sem.at[0])
+    load_grads.start()
+    load_gk = pltpu.make_async_copy(gk, gkv, sem.at[1])
+    load_gk.start()
+    take_out = pltpu.make_async_copy(out_tmp, outv, sem.at[2])
+    take_out.start()
     full[0] = jnp.zeros((8, C), F32)
-
-    def gather(j, _):
-        piece = back[j].astype(F32).reshape(9, 8, C)
-        full[8 * j] += piece[0]
-        full[pl.ds(8 * j + 1, 8)] = piece[1:]
-        return 0
-
-    lax.fori_loop(0, DEVS, gather, 0)
+    for g in range(groups):
+        load(g).wait()
+
+        def gather(n, _):
+            j = g * each + n
+            piece = backv[j].astype(F32).reshape(9, 8, C)
+            full[8 * j] += piece[0]
+            full[pl.ds(8 * j + 1, 8)] = piece[1:]
+            return 0
+
+        lax.fori_loop(0, each, gather, 0)
+    take_out.wait()
+    give_out = pltpu.make_async_copy(outv, out_ref, sem.at[2])
+    give_out.start()
     seam = full[0] + full[NLON // 8]
     full[0] = seam
     full[NLON // 8] = seam
-    full[NLON // 8 + 1 : NLON // 8 + 4 + span // 8] = full[1 : 4 + span // 8]
+    full[NLON // 8 + 1 : NLON // 8 + 2 + span // 8] = full[1 : 2 + span // 8]
     shift = shift_ref[0]
+
+    def emit_copy(r):
+        at = pl.ds(pl.multiple_of(r * span, span), span)
+        return pltpu.make_async_copy(rowsv.at[at], rows_ref.at[at], out_sem)
 
     def emit(r, _):
         start = lax.rem(r * span + NLON - shift, NLON) + 4
-        rows_ref[pl.ds(pl.multiple_of(r * span, span), span), :] = slide(full, start, span).astype(BF16)
+        first = lax.div(start, 8)
+        off = start - 8 * first
+        tiles = full[pl.ds(first, span // 8 + 1)]
+        moved = pltpu.roll(tiles, lax.rem(8 - off, 8), 1)
+        stays = lax.broadcasted_iota(jnp.int32, (span // 8, 8, C), 1) < 8 - off
+        rows = jnp.where(stays, moved[:-1], moved[1:]).reshape(span, C)
+        rowsv[pl.ds(pl.multiple_of(r * span, span), span), :] = rows.astype(BF16)
+        emit_copy(r).start()
         return 0
 
     lax.fori_loop(0, NLON // span, emit, 0)
-    gwi_ref[...] = scale * grads[0].reshape(C, FF).astype(F32)
-    gwo_ref[...] = (scale * grads[1].reshape(C, FF).astype(F32)).T
-    gk_ref[...] = scale * gk[:9]
-    copy.wait()
+    load_grads.wait()
+    gwiv[...] = scale * gradv[0].reshape(C, FF).astype(F32)
+    store_i = pltpu.make_async_copy(gwiv, gwi_ref, sem.at[3])
+    store_i.start()
+    gwov[...] = (scale * gradv[1].reshape(C, FF).astype(F32)).T
+    store_o = pltpu.make_async_copy(gwov, gwo_ref, sem.at[4])
+    store_o.start()
+    load_gk.wait()
+    gk_ref[...] = scale * gkv[:9]
+    pltpu.make_async_copy(rowsv, rows_ref, out_sem).wait()
+    store_i.wait()
+    store_o.wait()
+    give_out.wait()
 
 
 def shards(rows_in, row_shift, kernel, w_in, w_out, cotangent):
@@ -450,7 +527,7 @@
         in_specs=[smem, hbm, vmem, hbm, hbm, hbm],
         out_specs=(hbm, hbm, hbm, vmem),
         scratch_shapes=[
-            v((NLON, C), BF16), v((NLON // 8 + 12, 8, C), F32), v((DEVS, WIDE, C), BF16),
+            v((NLON // 8 + 12, 8, C), BF16), v((DEVS, WIDE, C), BF16), v((DEVS, WIDE, C), BF16),
             v((CHAINS, ROWS + 2, WIDE, C), BF16), v((CHAINS, ROWS, COLS, C), BF16),
             v((C, FF), BF16), v((FF, C), BF16), v((ROWS + 2, WIDE, C), F32),
             v((ROWS, COLS, C), F32), v((ROWS, COLS, 128), F32), v((ROWS, COLS, C), BF16),
@@ -459,15 +536,15 @@
             v((CHAINS, ROWS, COLS, C), BF16), v((2, C, FF), F32),
             v((32, 8, FF), BF16), v((32, 8, FF), BF16), v((32, 8, FF), BF16), v((32, 8, FF), BF16),
             v((8, FF), F32), v((8, FF), F32), v((2, 32, 8, FF), BF16),
-            v((16, C), F32), v((16, C), F32), v((DEVS, 16, C), F32),
-            dma((7,)), dma, dma((4,)), dma((4,)), dma((4,)), dma((4,)), dma((4,)), dma, dma, dma((4,)), dma((3,)),
-            dma, dma, dma, dma, dma, dma, dma, dma, dma, dma, dma, dma, dma, dma,
+            v((16, C), F32), v((16, C), F32), v((3, 4, 16, C), F32),
+            dma((8,)), dma, dma((4,)), dma((4,)), dma((4,)), dma((4,)), dma((4,)), dma, dma, dma((4,)), dma((4,)),
+            dma, dma, dma, dma, dma, dma, dma, dma, dma, dma, dma, dma, dma((3,)), dma((3,)),
         ],
         compiler_params=pltpu.CompilerParams(
             collective_id=0, has_side_effects=True, vmem_limit_bytes=58 << 20
         ),
         name="block",
-    )(row_shift, rows_in[0], kernel, w_in, w_out, cotangent.reshape(ROWS, CHAINS, COLS, C))
+    )(row_shift, rows_in.reshape(NLON // 8, 8, C), kernel, w_in, w_out, cotangent.reshape(ROWS, CHAINS, COLS, C))
     scale = 1.0 / math.sqrt(2 * DEVS * NLON)
     rows, out, grad_in, grad_out, grad_kernel = pl.pallas_call(
         lambda shift_ref, *refs: finish_kernel(shift_ref, scale, *refs),
@@ -478,10 +555,13 @@
             jax.ShapeDtypeStruct((FF, C), F32),
             jax.ShapeDtypeStruct((9, C), F32),
         ),
-        in_specs=[smem, vmem, hbm, vmem, vmem],
-        out_specs=(vmem, hbm, vmem, vmem, vmem),
-        scratch_shapes=[v((NLON // 8 + 36, 8, C), F32), dma],
-        compiler_params=pltpu.CompilerParams(vmem_limit_bytes=40 << 20),
+        in_specs=[smem, hbm, hbm, hbm, hbm],
+        out_specs=(hbm, hbm, hbm, hbm, vmem),
+        scratch_shapes=[
+            v((DEVS, WIDE, C), BF16), v((2, 32, 8, FF), BF16), v((16, C), F32), v((NLON, C), BF16),
+            v((ROWS, CHAINS, COLS, C), BF16), v((C, FF), F32), v((FF, C), F32), v((NLON // 8 + 34, 8, C), F32), dma((8,)), dma, dma((5,)),
+        ],
+        compiler_params=pltpu.CompilerParams(vmem_limit_bytes=58 << 20),
         name="finish",
     )(row_shift, back, out_tmp, grads, gk)
     return (

time: 145 us -> 128 us (0.88)
  Pallas kernels: 138 us -> 127 us
  local copies, waits for them, and re-layouts: 5.19 us -> 0 us
    pallas_call x1, Pallas kernels: 133 us -> 121 us  [shards(): pl.pallas_call(block_kernel, out_shape=(jax.ShapeDtypeStruct((ROWS, CHAIN...]
    unnamed x8 -> x0, local copies, waits for them, and re-layouts: 5.19 us -> none
    pallas_call x1, Pallas kernels: 4.58 us -> 6.04 us  [shards(): pl.pallas_call(lambda shift_ref, *refs: finish_kernel(shift_ref, scale, *...]
where the time goes in v2:
time: 128 us
  Pallas kernels  127 us (99%)
  between operations  1.29 us (1%)
    pallas_call x1, Pallas kernels, shards(): pl.pallas_call(block_kernel, out_shape=(jax.ShapeDtypeStruct((ROWS, CHAIN...  121 us
    pallas_call x1, Pallas kernels, shards(): pl.pallas_call(lambda shift_ref, *refs: finish_kernel(shift_ref, scale, *...  6.04 us

profile of v2, /device:TPU:1, one launch (start us, length us, event | category | flops | bytes accessed | tf_op | source)
XLA Modules:
  0.0 127.9 jit_solution(16668640007678372526)
XLA Ops:
  1.3 120.6 %block.1 = (bf16[16,4,64,256]{3,2,1,0:T(8,128)(2,1)}, bf16[64,72,256]{2,1,0:T(8,128)(2,1)}, bf16[2,32,8,1024]{3,2,1,0:T(8,128)(2,1)}, f32[16,256]{1,0:T(8,128)}) custom-call(s32[1]{0:T(128)S(6)} %copy.11.shift_ref, bf16[512,8,256]{2,1,0:T(8,128)(2,1)} %bitcast.4, f32[9,256]{1,0:T(8,128)} %taps.1, bf16[256,1024]{1,0:T(8,128)(2,1)} %w_in_hbm.1, ...), custom_call_target="tpu_custom_call" | custom-call | tf_op jit(solution)/shard_map/block/pallas_call | solution.py:519
  121.9 6.0 %finish.1 = (bf16[4096,256]{1,0:T(8,128)(2,1)}, bf16[16,4,64,256]{3,2,1,0:T(8,128)(2,1)}, f32[256,1024]{1,0:T(8,128)}, f32[1024,256]{1,0:T(8,128)}, f32[9,256]{1,0:T(8,128)}) custom-call(s32[1]{0:T(128)S(6)} %copy.11.shift_ref, bf16[64,72,256]{2,1,0:T(8,128)(2,1)} %get-tuple-element.14.refs_0_, bf16[16,4,64,256]{3,2,1,0:T(8,128)(2,1)} %get-tuple-element.15.refs_1_, ...), custom_call_target="tpu_custom_call" | custom-call | tf_op jit(solution)/shard_map/finish/pallas_call | solution.py:549

commit v3 on v2

--- a/solution.py
+++ b/solution.py
@@ -213,7 +213,7 @@
             normed[t] = n.astype(BF16)
             return 0
 
-        lax.fori_loop(0, ROWS, row, 0)
+        lax.fori_loop(0, ROWS, row, 0, unroll=2)
 
     def mlp(q):
         def step(h, _):
@@ -265,7 +265,7 @@
                     new.append(sums[3 * a + b] + jnp.sum(prod.reshape(COLS // 8, 8, C), axis=0))
             return tuple(new)
 
-        sums = lax.fori_loop(0, ROWS, row, sums)
+        sums = lax.fori_loop(0, ROWS, row, sums, unroll=2)
         ghalo_s[q] = gdp[buf, edge, 8 : 8 + COLS, :].astype(BF16)
         return sums
 
@@ -314,14 +314,18 @@
         def _():
             conv_back(chain_of(u - 1), 1 - buf)
 
+        @pl.when(u == 0)
+        def _():
+            send_phase(2)
+
         mlp(q)
         arrive(u + 1)
         sums = norm_back(q, buf, sums)
         ghalo_copy(q).start()
 
-        @pl.when(u < CHAINS - 2)
+        @pl.when(u == 0)
         def _():
-            send_phase(u + 2)
+            send_phase(3)
 
         return sums
 

time: 128 us -> 117 us (0.914)
  Pallas kernels: 127 us -> 115 us
    pallas_call x1, Pallas kernels: 121 us -> 109 us  [shards(): pl.pallas_call(block_kernel, out_shape=(jax.ShapeDtypeStruct((ROWS, CHAIN...]
where the time goes in v3:
time: 117 us; the launch traced here: 116 us
  Pallas kernels  115 us (98%)
  between operations  1.29 us (1%)
    pallas_call x1, Pallas kernels, shards(): pl.pallas_call(block_kernel, out_shape=(jax.ShapeDtypeStruct((ROWS, CHAIN...  109 us
    pallas_call x1, Pallas kernels, shards(): pl.pallas_call(lambda shift_ref, *refs: finish_kernel(shift_ref, scale, *...  6.04 us

profile of v3, /device:TPU:1, one launch (start us, length us, event | category | flops | bytes accessed | tf_op | source)
XLA Modules:
  0.0 116.4 jit_solution(10279753568701748749)
XLA Ops:
  1.3 109.1 %block.1 = (bf16[16,4,64,256]{3,2,1,0:T(8,128)(2,1)}, bf16[64,72,256]{2,1,0:T(8,128)(2,1)}, bf16[2,32,8,1024]{3,2,1,0:T(8,128)(2,1)}, f32[16,256]{1,0:T(8,128)}) custom-call(s32[1]{0:T(128)S(6)} %copy.11.shift_ref, bf16[512,8,256]{2,1,0:T(8,128)(2,1)} %bitcast.4, f32[9,256]{1,0:T(8,128)} %taps.1, bf16[256,1024]{1,0:T(8,128)(2,1)} %w_in_hbm.1, ...), custom_call_target="tpu_custom_call" | custom-call | tf_op jit(solution)/shard_map/block/pallas_call | solution.py:523
  110.3 6.0 %finish.1 = (bf16[4096,256]{1,0:T(8,128)(2,1)}, bf16[16,4,64,256]{3,2,1,0:T(8,128)(2,1)}, f32[256,1024]{1,0:T(8,128)}, f32[1024,256]{1,0:T(8,128)}, f32[9,256]{1,0:T(8,128)}) custom-call(s32[1]{0:T(128)S(6)} %copy.11.shift_ref, bf16[64,72,256]{2,1,0:T(8,128)(2,1)} %get-tuple-element.14.refs_0_, bf16[16,4,64,256]{3,2,1,0:T(8,128)(2,1)} %get-tuple-element.15.refs_1_, ...), custom_call_target="tpu_custom_call" | custom-call | tf_op jit(solution)/shard_map/finish/pallas_call | solution.py:553

commit v4 on v3

--- a/solution.py
+++ b/solution.py
@@ -23,7 +23,7 @@
 ROWS = 16
 COLS = 64
 WIDE = COLS + 8
-CHUNK = 512
+CHUNK = 1024
 STEP_ROWS = CHUNK // COLS
 
 

time: 117 us -> 116 us (level)
  no operation moved by 1% of the time
where the time goes in v4:
time: 116 us
  Pallas kernels  114 us (98%)
  between operations  1.29 us (1%)
    pallas_call x1, Pallas kernels, shards(): pl.pallas_call(block_kernel, out_shape=(jax.ShapeDtypeStruct((ROWS, CHAIN...  108 us
    pallas_call x1, Pallas kernels, shards(): pl.pallas_call(lambda shift_ref, *refs: finish_kernel(shift_ref, scale, *...  6.04 us

profile of v4, /device:TPU:1, one launch (start us, length us, event | category | flops | bytes accessed | tf_op | source)
XLA Modules:
  0.0 115.5 jit_solution(15505532300642789533)
XLA Ops:
  1.3 108.2 %block.1 = (bf16[16,4,64,256]{3,2,1,0:T(8,128)(2,1)}, bf16[64,72,256]{2,1,0:T(8,128)(2,1)}, bf16[2,32,8,1024]{3,2,1,0:T(8,128)(2,1)}, f32[16,256]{1,0:T(8,128)}) custom-call(s32[1]{0:T(128)S(6)} %copy.11.shift_ref, bf16[512,8,256]{2,1,0:T(8,128)(2,1)} %bitcast.4, f32[9,256]{1,0:T(8,128)} %taps.1, bf16[256,1024]{1,0:T(8,128)(2,1)} %w_in_hbm.1, ...), custom_call_target="tpu_custom_call" | custom-call | tf_op jit(solution)/shard_map/block/pallas_call | solution.py:523
  109.5 6.0 %finish.1 = (bf16[4096,256]{1,0:T(8,128)(2,1)}, bf16[16,4,64,256]{3,2,1,0:T(8,128)(2,1)}, f32[256,1024]{1,0:T(8,128)}, f32[1024,256]{1,0:T(8,128)}, f32[9,256]{1,0:T(8,128)}) custom-call(s32[1]{0:T(128)S(6)} %copy.11.shift_ref, bf16[64,72,256]{2,1,0:T(8,128)(2,1)} %get-tuple-element.14.refs_0_, bf16[16,4,64,256]{3,2,1,0:T(8,128)(2,1)} %get-tuple-element.15.refs_1_, ...), custom_call_target="tpu_custom_call" | custom-call | tf_op jit(solution)/shard_map/finish/pallas_call | solution.py:553
